TPU v7x, 32 devices: a whole 2x2x4 slice. The times are simulated.
32 devices in a mesh: gx: 4 (over z), gy: 2 (over y), gz: 4 (over x, core).
Axes of the slice: x: 2, y: 2, z: 4, core: 2. Of those that a mesh axis runs over, the one named last changes fastest.
Arguments:
- bodies: float32 [1920, 4, 128], P(('gx', 'gy', 'gz'))
- velocity: float32 [1920, 3, 128], P(('gx', 'gy', 'gz')), may hold values from -6 to 6
- select: int32 [32, 5, 16], P(('gx', 'gy', 'gz')), may hold values from 0 to 123, as said below
- pair_target: int32 [32, 1024], P(('gx', 'gy', 'gz')), may hold values from 0 to 59
- pair_source: int32 [32, 1024], P(('gx', 'gy', 'gz')), may hold values from 0 to 139
- counts: int32 [32], P(('gx', 'gy', 'gz')), may hold values from 256 to 1024, as said below
- departures: int32 [32, 12], P(('gx', 'gy', 'gz')), may hold values from 0 to 59, as said below
- owners: int32 [384, 1], P(('gx', 'gy', 'gz')), may hold values from 0 to 3; in each aligned block of 12 rows (0 to 11, 12 to 23, ...) at most 6 rows name the same one
Outputs:
- resident: float32 [1920, 7, 128], P(('gx', 'gy', 'gz'))
- moved_in: float32 [768, 7, 128], P(('gx', 'gy', 'gz'))
Inputs may be any that keep to these rules, and one draw needn't show every extreme that they name: `select`: at step k every entry is below 60 + k * 16, and each list names the block 60 + k * 16 - 1. `counts`: some device has 1024 live pairs. `departures`: entries of one device are distinct. `owners`: no owner gets more than 6 blocks from one device, and that many in some devices.
All inputs are finite; a program needn't handle non-finite values.
Results may differ from a plain program's by a relative error of at most 0.0003.
Values sent between devices are 32-bit elements; how exact they have to be, the bound alone decides.
A program may use at most 64 MiB of HBM per device.

v0:
```python
import functools
import math

import jax
import jax.numpy as jnp
from jax import lax
from jax.experimental import pallas as pl
from jax.experimental.pallas import tpu as pltpu
from jax.sharding import PartitionSpec as P

soften = 0.01
timestep = 0.25
deepest_unroll = 32


def exchange_kernel(steps, select_ref, bodies_ref, pool_ref, outgoing, arriving, send_sem, recv_sem):
    own_blocks = bodies_ref.shape[0]
    send_count = outgoing.shape[1]
    partners = []
    for axis, stride in steps:
        me = lax.axis_index(axis)
        side = lax.rem(me // stride, 2)
        partners.append({axis: me + (1 - 2 * side) * stride})
    barrier = pltpu.get_barrier_semaphore()
    for partner in partners:
        pl.semaphore_signal(
            barrier, inc=1, device_id=partner, device_id_type=pl.DeviceIdType.MESH
        )
    pool_ref[0:own_blocks] = bodies_ref[...]
    pl.semaphore_wait(barrier, len(partners))
    copies = []
    for k, partner in enumerate(partners):
        for j in range(send_count):
            outgoing[k, j] = pool_ref[select_ref[k, 0, j]]
        copy = pltpu.make_async_remote_copy(
            src_ref=outgoing.at[k],
            dst_ref=arriving.at[k],
            send_sem=send_sem.at[k],
            recv_sem=recv_sem.at[k],
            device_id=partner,
            device_id_type=pl.DeviceIdType.MESH,
        )
        copy.start()
        copies.append(copy)
        copy.wait_recv()
        base = own_blocks + k * send_count
        pool_ref[base : base + send_count] = arriving[k]
    for copy in copies:
        copy.wait_send()


def split(values):
    high = jnp.clip(values, -3.38e38, 3.38e38).astype(jnp.bfloat16).astype(jnp.float32)
    rest = values - high
    middle = rest.astype(jnp.bfloat16).astype(jnp.float32)
    return high, middle, rest - middle


def step_kernel(
    slot_total,
    target_ref,
    source_ref,
    count_ref,
    departures_ref,
    owners_ref,
    pool_ref,
    velocity_ref,
    resident_ref,
    outbox_ref,
    sources,
    targets,
    accel,
    used,
):
    pool_size = pool_ref.shape[0]
    own_blocks = velocity_ref.shape[1]
    span = pool_ref.shape[2]
    unroll = math.gcd(target_ref.shape[0], deepest_unroll)

    row = lax.broadcasted_iota(jnp.int32, (12, 4 * span), 0)
    lane = lax.broadcasted_iota(jnp.int32, (12, 4 * span), 1)
    picks = (row % 4 == lane // span).astype(jnp.float32)
    ones = (lax.broadcasted_iota(jnp.int32, (4, span), 0) < 3).astype(jnp.float32)

    batch = math.gcd(pool_size, 10)

    @pl.loop(0, pool_size // batch)
    def _(group):
        for b in [group * batch + u for u in range(batch)]:
            pieces = split(pool_ref[b])
            sources[b] = jnp.concatenate([*pieces, ones], axis=0).T.astype(jnp.bfloat16)

    own_batch = math.gcd(own_blocks, 12)

    @pl.loop(0, own_blocks // own_batch)
    def _(group):
        for b in [group * own_batch + u for u in range(own_batch)]:
            nothing = jnp.zeros((1, span), jnp.float32)
            rows = [
                jnp.concatenate([-piece[0:1], -piece[1:2], -piece[2:3], nothing], axis=1)
                for piece in split(pool_ref[b])
            ]
            rows.append(jnp.zeros((1, 4 * span), jnp.float32))
            targets[b] = jnp.concatenate([picks, *rows], axis=0).astype(jnp.bfloat16)

    targets[own_blocks] = jnp.zeros(targets.shape[1:], jnp.bfloat16)
    accel[...] = jnp.zeros_like(accel)

    @pl.loop(0, (count_ref[0] + unroll - 1) // unroll)
    def _(group):
        for u in range(unroll):
            t = jnp.where(group * unroll + u < count_ref[0], target_ref[group * unroll + u], own_blocks)
            s = source_ref[group * unroll + u]
            gaps = jnp.dot(sources[s], targets[t], preferred_element_type=jnp.float32)
            ax = ay = az = None
            for g in range(0, span, 8):
                dx = gaps[g : g + 8, 0:span]
                dy = gaps[g : g + 8, span : 2 * span]
                dz = gaps[g : g + 8, 2 * span : 3 * span]
                mass = gaps[g : g + 8, 3 * span :]
                inverse = lax.rsqrt(dx * dx + dy * dy + (dz * dz + soften))
                w = (mass * inverse) * (inverse * inverse)
                if ax is None:
                    ax, ay, az = dx * w, dy * w, dz * w
                else:
                    ax, ay, az = ax + dx * w, ay + dy * w, az + dz * w
            accel[t, 0] += ax
            accel[t, 1] += ay
            accel[t, 2] += az

    @pl.loop(0, own_blocks // own_batch)
    def _(group):
        for b in [group * own_batch + u for u in range(own_batch)]:
            row = pl.ds(b, 1)
            for c in range(3):
                pull = jnp.sum(accel[b, c], axis=0, keepdims=True)
                velocity_new = velocity_ref[c, row, :] + timestep * pull
                resident_ref[c, row, :] = pool_ref[b, c : c + 1, :] + timestep * velocity_new
                resident_ref[4 + c, row, :] = velocity_new
            resident_ref[3, row, :] = pool_ref[b, 3:4, :]

    outbox_ref[...] = jnp.zeros_like(outbox_ref)
    for g in range(used.shape[0]):
        used[g] = 0
    for m in range(departures_ref.shape[0]):
        d = departures_ref[m]
        owner = owners_ref[m]
        slot = used[owner]
        used[owner] = slot + 1
        for c in range(resident_ref.shape[0]):
            outbox_ref[owner * slot_total + slot, c : c + 1, :] = resident_ref[c, pl.ds(d, 1), :]
            resident_ref[c, pl.ds(d, 1), :] = jnp.zeros((1, span), jnp.float32)


def on_device(bodies, velocity, select, pair_target, pair_source, counts, departures, owners):
    own_blocks = bodies.shape[0]
    span = bodies.shape[2]
    smem = pl.BlockSpec(memory_space=pltpu.SMEM)
    vmem = pl.BlockSpec(memory_space=pltpu.VMEM)
    steps = [
        (axis, 2**bit)
        for axis in ("gx", "gy", "gz")
        for bit in range(lax.axis_size(axis).bit_length() - 1)
    ]
    send_count = select.shape[2]
    slab = pltpu.VMEM((len(steps), send_count, 4, span), jnp.float32)
    pool = pl.pallas_call(
        functools.partial(exchange_kernel, steps),
        out_shape=jax.ShapeDtypeStruct((own_blocks + len(steps) * send_count, 4, span), jnp.float32),
        in_specs=[smem, vmem],
        out_specs=vmem,
        scratch_shapes=[
            slab,
            slab,
            pltpu.SemaphoreType.DMA((len(steps),)),
            pltpu.SemaphoreType.DMA((len(steps),)),
        ],
        compiler_params=pltpu.CompilerParams(collective_id=0, has_side_effects=True),
        name="exchange",
    )(jnp.transpose(select, (1, 0, 2)), bodies)
    group_size = lax.axis_size("gz")
    move_count = departures.shape[1]
    slot_total = max(2, 2 * move_count // group_size)
    resident, outbox = pl.pallas_call(
        functools.partial(step_kernel, slot_total),
        out_shape=(
            jax.ShapeDtypeStruct((7, own_blocks, span), jnp.float32),
            jax.ShapeDtypeStruct((group_size * slot_total, 7, span), jnp.float32),
        ),
        in_specs=[smem] * 5 + [vmem] * 2,
        out_specs=(vmem, vmem),
        scratch_shapes=[
            pltpu.VMEM((pool.shape[0], span, 16), jnp.bfloat16),
            pltpu.VMEM((own_blocks + 1, 16, 4 * span), jnp.bfloat16),
            pltpu.VMEM((own_blocks + 1, 3, 8, span), jnp.float32),
            pltpu.SMEM((group_size,), jnp.int32),
        ],
        name="gravity",
    )(
        pair_target[0],
        pair_source[0],
        counts,
        departures[0],
        owners[:, 0],
        pool,
        jnp.transpose(velocity, (1, 0, 2)),
    )
    arrived = lax.all_to_all(
        outbox.reshape(group_size, slot_total, 7, span), "gz", split_axis=0, concat_axis=0, tiled=True
    )
    return jnp.transpose(resident, (1, 0, 2)), arrived.reshape(group_size * slot_total, 7, span)


def solution(mesh):
    everywhere = ("gx", "gy", "gz")
    cube = P(everywhere, None, None)
    flat = P(everywhere, None)
    return jax.shard_map(
        on_device,
        mesh=mesh,
        in_specs=(cube, cube, cube, flat, flat, P(everywhere), flat, flat),
        out_specs=(cube, cube),
        check_vma=False,
    )
```

profile of v0, /device:TPU:0, one launch (start us, length us, event | category | flops | bytes accessed | tf_op | source)
XLA Modules:
  0.0 72.8 jit_solution(17923999762185582189)
XLA Ops:
  1.3 18.6 %exchange.1.pool_ref = f32[140,4,128]{2,1,0:T(4,128)} custom-call(s32[5,1,16]{2,1,0:T(1,128)} %bitcast.14, f32[60,4,128]{2,1,0:T(4,128)} %bodies_ref.1), custom_call_target="tpu_custom_call" | custom-call | tf_op jit(solution)/shard_map/exchange/pallas_call | solution.py:167
  19.9 29.9 %gravity.1 = (f32[7,60,128]{2,1,0:T(8,128)}, f32[24,7,128]{2,1,0:T(8,128)}) custom-call(s32[1024]{0:T(1024)} %bitcast.12, s32[1024]{0:T(1024)} %bitcast.13, s32[1]{0:T(128)S(6)} %copy.12.count_ref, s32[12]{0:T(128)} %bitcast.15, s32[12]{0:T(128)} %bitcast.16, f32[140,4,128]{2,1,0:T(4,128)} %exchange.1.pool_ref, f32[3,60,128]{2,1,0:T(8,128)} %bitcast.11), custom_call_target="tpu_custom_call" | custom-call | tf_op jit(solution)/shard_map/gravity/pallas_call | solution.py:184
  49.8 22.3 %all_to_all.5 = f32[4,6,7,128]{3,2,1,0:T(8,128)S(1)} all-to-all(f32[4,6,7,128]{3,2,1,0:T(8,128)} %bitcast.10), channel_id=1, replica_groups=mesh['gx'=4,'gy'=2,'gz'=4] {'gz'}, dimensions={0} | all-to-all | bytes 172032 | tf_op jit(solution)/shard_map/all_to_all | solution.py:208
  72.1 0.7 copy.11
where the time goes:
time: 73 us; the launch traced here: 72.8 us
  Pallas kernels  48.5 us (66%)
  blocking collectives  22.3 us (31%)
  between operations  1.29 us (2%)
    pallas_call x1, Pallas kernels, on_device(): pl.pallas_call(functools.partial(step_kernel, slot_total), out_shape=(jax...  29.9 us
    all_to_all x1, blocking collectives, on_device(): lax.all_to_all(outbox.reshape(group_size, slot_total, 7, span), 'gz', spl...  22.3 us
    pallas_call x1, Pallas kernels, on_device(): pl.pallas_call(functools.partial(exchange_kernel, steps), out_shape=jax.S...  18.6 us

commit v1 on v0

--- a/solution.py
+++ b/solution.py
@@ -10,7 +10,7 @@
 
 soften = 0.01
 timestep = 0.25
-deepest_unroll = 32
+deepest_unroll = 64
 
 
 def exchange_kernel(steps, select_ref, bodies_ref, pool_ref, outgoing, arriving, send_sem, recv_sem):

time: 73 us -> 70.8 us (0.970)
  Pallas kernels: 48.5 us -> 37.7 us
  blocking collectives: 22.3 us -> 30.9 us
    pallas_call x1, Pallas kernels: 29.9 us -> 19.1 us  [on_device(): pl.pallas_call(functools.partial(step_kernel, slot_total), out_shape=(jax...]
    all_to_all x1, blocking collectives: 22.3 us -> 30.9 us  [on_device(): lax.all_to_all(outbox.reshape(group_size, slot_total, 7, span), 'gz', spl...]
where the time goes in v1:
time: 70.8 us; the launch traced here: 70.5 us
  Pallas kernels  37.7 us (53%)
  blocking collectives  30.9 us (44%)
  between operations  1.29 us (2%)
    all_to_all x1, blocking collectives, on_device(): lax.all_to_all(outbox.reshape(group_size, slot_total, 7, span), 'gz', spl...  30.9 us
    pallas_call x1, Pallas kernels, on_device(): pl.pallas_call(functools.partial(step_kernel, slot_total), out_shape=(jax...  19.1 us
    pallas_call x1, Pallas kernels, on_device(): pl.pallas_call(functools.partial(exchange_kernel, steps), out_shape=jax.S...  18.6 us

profile of v1, /device:TPU:0, one launch (start us, length us, event | category | flops | bytes accessed | tf_op | source)
XLA Modules:
  0.0 70.5 jit_solution(1029625126749446441)
XLA Ops:
  1.3 18.6 %exchange.1.pool_ref = f32[140,4,128]{2,1,0:T(4,128)} custom-call(s32[5,1,16]{2,1,0:T(1,128)} %bitcast.14, f32[60,4,128]{2,1,0:T(4,128)} %bodies_ref.1), custom_call_target="tpu_custom_call" | custom-call | tf_op jit(solution)/shard_map/exchange/pallas_call | solution.py:167
  19.9 19.1 %gravity.1 = (f32[7,60,128]{2,1,0:T(8,128)}, f32[24,7,128]{2,1,0:T(8,128)}) custom-call(s32[1024]{0:T(1024)} %bitcast.12, s32[1024]{0:T(1024)} %bitcast.13, s32[1]{0:T(128)S(6)} %copy.12.count_ref, s32[12]{0:T(128)} %bitcast.15, s32[12]{0:T(128)} %bitcast.16, f32[140,4,128]{2,1,0:T(4,128)} %exchange.1.pool_ref, f32[3,60,128]{2,1,0:T(8,128)} %bitcast.11), custom_call_target="tpu_custom_call" | custom-call | tf_op jit(solution)/shard_map/gravity/pallas_call | solution.py:184
  39.0 30.9 %all_to_all.5 = f32[4,6,7,128]{3,2,1,0:T(8,128)S(1)} all-to-all(f32[4,6,7,128]{3,2,1,0:T(8,128)} %bitcast.10), channel_id=1, replica_groups=mesh['gx'=4,'gy'=2,'gz'=4] {'gz'}, dimensions={0} | all-to-all | bytes 172032 | tf_op jit(solution)/shard_map/all_to_all | solution.py:208
  69.8 0.7 copy.11
